TPU v7x, 128 devices: a whole 4x4x4 slice. The times are simulated.
128 devices in a mesh: panel: 4 (over x_lo, core), obs: 32 (over y, z, x_hi).
Axes of the slice: x: 4 (x_hi: 2, x_lo: 2; x = x_hi * 2 + x_lo), y: 4, z: 4, core: 2. Of those that a mesh axis runs over, the one named last changes fastest.
Arguments:
- les_rows: bfloat16 [16384, 2, 128], P(('panel', 'obs')), may hold values from -6 to 6
- les_dest: int32 [16384, 1], P(('panel', 'obs')), may hold values from 0 to 127; in each aligned block of 128 rows (0 to 127, 128 to 255, ...) at most 2 rows name the same one
- loading_weight: bfloat16 [32768, 4096], P('panel', 'obs'), may hold values from -0.046875 to 0.046875
- thickness_weight: bfloat16 [32768, 4096], P('panel', 'obs'), may hold values from -0.046875 to 0.046875
- delays: int32 [64, 32], P('panel', 'obs'), may hold values from 0 to 64
Outputs:
- acoustic_pressure: float32 [128, 4096], P('panel', 'obs')
Inputs may be any that keep to these rules, and one draw needn't show every extreme that they name: `les_dest`: in the aligned blocks of 128 rows of one LES owner, no destination is named by more than 2 rows, a bound that some block reaches; every destination is named by some row.
All inputs are finite; a program needn't handle non-finite values.
Results may differ from a plain program's by a relative error of at most 0.0018.
Values may be sent and summed in bfloat16 or wider, within the bound.
A program may use at most 64 MiB of HBM per device.

v0:
```python
import jax
import jax.numpy as jnp
from jax import lax
from jax.sharding import PartitionSpec as P

PBLK = 512


def owner_ranks(dest_block, count):
    onehot = (dest_block[:, :, None] == jnp.arange(count, dtype=jnp.int32)[None, None, :]).astype(
        jnp.int32
    )
    earlier = jnp.cumsum(onehot, axis=1) - onehot
    return jnp.sum(earlier * onehot, axis=2)


def delay_block(block, delay):
    steps = block.shape[0]
    padded = jnp.concatenate([jnp.zeros_like(block), block], axis=0)
    start = steps - delay
    return lax.dynamic_slice_in_dim(padded, start, steps, 0)


def shift_time(values, delay_row):
    steps = values.shape[0]
    blocks = delay_row.shape[0]
    shaped = values.reshape(steps, blocks, -1)
    moved = jax.vmap(delay_block, in_axes=(1, 0), out_axes=1)(shaped, delay_row)
    return moved.reshape(steps, -1)


def per_device(les_rows, les_dest, loading_weight, thickness_weight, delays):
    n_panel = lax.axis_size("panel")
    n_obs = lax.axis_size("obs")
    count = n_panel * n_obs
    rows_dev = les_rows.shape[0]
    steps = les_rows.shape[2]
    cap = 2 * rows_dev // count
    dest = les_dest[:, 0]
    rank = owner_ranks(dest.reshape(1, rows_dev), count)[0]
    position = dest * cap + rank
    buffer = jnp.zeros((count * cap, 2, steps), les_rows.dtype).at[position].set(les_rows)
    arrived = lax.all_to_all(
        buffer.reshape(count, cap, 2, steps),
        ("panel", "obs"),
        split_axis=0,
        concat_axis=0,
        tiled=True,
    )
    local = arrived.reshape(count * cap, 2, steps)
    group = lax.all_gather(local, "obs", axis=0, tiled=True)
    velocity = group[:, 1, :].astype(jnp.float32)
    padded = jnp.pad(velocity, ((0, 0), (1, 1)))
    rate = ((padded[:, 2:] - padded[:, :-2]) * 0.5).astype(jnp.bfloat16)
    pressure_src = group[:, 0, :]
    nblocks = group.shape[0] // PBLK
    width = loading_weight.shape[1]
    press_blocks = pressure_src.reshape(nblocks, PBLK, steps)
    rate_blocks = rate.reshape(nblocks, PBLK, steps)
    load_blocks = loading_weight.reshape(nblocks, PBLK, width)
    thick_blocks = thickness_weight.reshape(nblocks, PBLK, width)

    def one_block(total, inputs):
        press_b, rate_b, load_b, thick_b, delay_b = inputs
        dims = (((0,), (0,)), ((), ()))
        term = lax.dot_general(press_b, load_b, dims, preferred_element_type=jnp.float32)
        term = term + lax.dot_general(rate_b, thick_b, dims, preferred_element_type=jnp.float32)
        return (total + shift_time(term, delay_b), None)

    start = jnp.zeros((steps, width), jnp.float32)
    partial_sum, unused = lax.scan(
        one_block, start, (press_blocks, rate_blocks, load_blocks, thick_blocks, delays)
    )
    return lax.psum_scatter(partial_sum, "panel", scatter_dimension=0, tiled=True)


def solution(mesh):
    placed = (
        P(("panel", "obs"), None, None),
        P(("panel", "obs"), None),
        P("panel", "obs"),
        P("panel", "obs"),
        P("panel", "obs"),
    )
    return jax.shard_map(
        per_device, mesh=mesh, in_specs=placed, out_specs=P("panel", "obs"), check_vma=False
    )
```

profile of v0, /device:TPU:1, one launch (start us, length us, event | category | flops | bytes accessed | tf_op | source)
XLA Modules:
  0.0 224.5 jit_solution(12010484477741862659)
XLA Ops:
  6.5 0.7 fusion.16
  7.5 0.8 select_reduce_fusion
  8.3 0.7 fusion.17
  9.0 9.7 %scatter_fusion = bf16[256,2,128]{2,1,0:T(2,128)(2,1)S(1)} fusion(bf16[256,2,128]{2,1,0:T(2,128)(2,1)S(1)} %broadcast_in_dim.15, s32[128]{0:T(128)S(1)} %fusion.17, bf16[128,2,128]{2,1,0:T(2,128)(2,1)} %param.7), kind=kCustom, calls=%fused_computation | custom fusion | bytes 197120 | tf_op jit(solution)/shard_map/scatter | solution.py:42
  18.8 21.3 %all_to_all.5 = bf16[128,2,2,128]{3,2,1,0:T(2,128)(2,1)S(1)} all-to-all(bf16[128,2,2,128]{3,2,1,0:T(2,128)(2,1)S(1)} %bitcast.56), channel_id=1, replica_groups=mesh['panel'=4,'obs'=32] {'panel','obs'}, dimensions={0} | all-to-all | bytes 262144 | tf_op jit(solution)/shard_map/all_to_all | solution.py:43
  40.0 0.7 copy.6
  40.8 75.2 %all-gather.2.cloned.1.call-done = bf16[8192,2,128]{2,0,1:T(8,128)(2,1)} async-done(((bf16[256,2,128]{2,0,1:T(8,128)(2,1)}), bf16[8192,2,128]{2,0,1:T(8,128)(2,1)}) %all-gather.2.cloned.1.call-update) | async-done | bytes 4194320 | tf_op jit(solution)/shard_map/all_gather | solution.py:51
  116.0 3.8 %slice_bitcast_fusion = (bf16[8192,128]{1,0:T(8,128)(2,1)S(1)}, bf16[8192,1,128]{2,0,1:T(8,128)(2,1)}) fusion(bf16[8192,2,128]{2,0,1:T(8,128)(2,1)} %all-gather.2.cloned.1.call-done), kind=kLoop, calls=%fused_computation.22 | loop fusion | bytes 8388608 | tf_op jit(solution)/shard_map/convert_element_type | solution.py:52
  119.8 1.2 pad_convert_fusion
  121.1 1.1 fusion.15
  122.2 77.3 %while.14 = (s32[]{:T(128)}, f32[128,128]{1,0:T(8,128)S(1)}, bf16[16,512,128]{2,1,0:T(8,128)(2,1)}, bf16[16,512,128]{2,1,0:T(8,128)(2,1)}, bf16[16,512,128]{2,1,...) while((s32[]{:T(128)}, f32[128,128]{1,0:T(8,128)S(1)}, ...), condition=%wide.region_4.5_spmd.clone, body=%wide.region_3.4_spmd.clone.sunk | while | flops 33603588 | bytes 919725 | solution.py:71
  122.2 0.7 fusion.31
  124.6 1.2 fusion.32
  125.8 1.1 fusion.33
  127.1 0.7 fusion.31
  129.5 1.2 fusion.32
  130.7 1.1 fusion.33
  134.3 1.2 fusion.32
  135.5 1.1 fusion.33
  139.1 1.2 fusion.32
  140.3 1.1 fusion.33
  144.0 1.2 fusion.32
  145.2 1.1 fusion.33
  148.8 1.2 fusion.32
  150.0 1.1 fusion.33
  153.6 1.2 fusion.32
  154.8 1.1 fusion.33
  158.5 1.2 fusion.32
  159.7 1.1 fusion.33
  163.3 1.2 fusion.32
  164.5 1.1 fusion.33
  168.1 1.2 fusion.32
  169.3 1.1 fusion.33
  172.9 1.2 fusion.32
  174.1 1.1 fusion.33
  177.8 1.2 fusion.32
  179.0 1.1 fusion.33
  182.6 1.2 fusion.32
  183.8 1.1 fusion.33
  187.4 1.2 fusion.32
  188.6 1.1 fusion.33
  189.9 0.7 fusion.31
  192.3 1.2 fusion.32
  193.5 1.1 fusion.33
  194.7 0.7 fusion.31
  197.1 1.2 fusion.32
  198.3 1.1 fusion.33
  200.2 17.5 %reduce-scatter.2.cloned.1.call-done = f32[32,128]{1,0:T(8,128)} async-done(((f32[128,128]{1,0:T(8,128)}), f32[32,128]{1,0:T(8,128)}) %reduce-scatter.2.cloned.1.call-update) | async-done | bytes 16400 | tf_op jit(solution)/shard_map/reduce_scatter | solution.py:74
  (39 shorter events, 9.6 us)
Async XLA Ops:
  6.5 109.5 %all-gather.2.cloned.1.call-start = ((), (), s32[]{:S(2)}) async-start(), calls=%async_computation.2 | async-start | bytes 4325376 | tf_op jit(solution)/shard_map/all_gather | solution.py:51
  40.7 176.9 %reduce-scatter.2.cloned.1.call-start = ((), (), s32[]{:S(2)}) async-start(), calls=%async_computation.3 | async-start | bytes 81920 | tf_op jit(solution)/shard_map/reduce_scatter | solution.py:74
  121.0 1.2 copy-start.1
  199.5 0.6 copy-start
Sparse Core Ops, SparseCore 0:
  40.8 75.1 all-gather.1
  200.3 17.2 reduce-scatter.1
where the time goes:
time: 226 us; the launch traced here: 224 us
  waiting for transfers between devices  92.7 us (41%)
  matrix products  37.2 us (16%)
  loops' own time  28.7 us (13%)
  blocking collectives  21.3 us (9%)
  other arithmetic  16 us (7%)
  local copies, waits for them, and re-layouts  14.9 us (7%)
  between operations  13.5 us (6%)
    all_gather x1, waiting for transfers between devices, per_device(): group = lax.all_gather(local, 'obs', axis=0, tiled=True)  75.2 us
    another operation x1, loops' own time, per_device(): lax.scan(one_block, start, (press_blocks, rate_blocks, load_blocks, thick...  28.7 us
    all_to_all x1, blocking collectives, per_device(): lax.all_to_all(buffer.reshape(count, cap, 2, steps), ('panel', 'obs'), sp...  21.3 us
    dot_general x16, matrix products, one_block(): lax.dot_general(press_b, load_b, dims, preferred_element_type=jnp.float32)  19.1 us
    dot_general x16, matrix products, one_block(): lax.dot_general(rate_b, thick_b, dims, preferred_element_type=jnp.float32)  18.2 us
    reduce_scatter x1, waiting for transfers between devices, per_device(): lax.psum_scatter(partial_sum, 'panel', scatter_dimension=0, tiled=True)  17.5 us
    sub x16, other arithmetic, delay_block(): start = steps - delay  10.4 us
    scatter x1, local copies, waits for them, and re-layouts, per_device(): jnp.zeros((count * cap, 2, steps), les_rows.dtype).at[position]  9.74 us
  transfers between devices with their start and end apart: 2, of which 2 were waited for; matrix products, arithmetic and copies ran while one was open for 0% of the time, Pallas kernels for 0%

commit v1 on v0

v1 whole, which is shorter than its diff:
```python
import itertools

import jax
import jax.numpy as jnp
import numpy as np
from jax import lax
from jax.experimental import pallas as pl
from jax.experimental.pallas import tpu as pltpu
from jax.sharding import PartitionSpec as P

MESH = pl.DeviceIdType.MESH
RING = 4
CHIPS = RING**3
CHUNK = 8
CHUNKS = CHIPS // CHUNK
RELAY = 4

HOPS = (0, 1, 2, 1)
OFFSETS = sorted(itertools.product(range(RING), repeat=3), key=lambda o: (sum(HOPS[v] for v in o), o))
PLACE = {offset: n for n, offset in enumerate(OFFSETS)}


def routes(offset):
    found = []
    moved = [i for i in range(3) if offset[i]]
    for axis in range(3):
        others = [i for i in moved if i != axis]
        classes = [k for k in range(3) if all((i - k) % 3 < (axis - k) % 3 for i in others)]
        if not classes:
            continue
        if offset[axis] == 0:
            steps = (1, 3)
        else:
            parity = (axis + sum(offset[i] for i in range(3) if i != axis)) % 2
            turn = 1 if parity == 0 else 3
            steps = (turn,) if offset[axis] == turn else ()
        for step in steps:
            found.append((axis, step, classes))
    return found


EDGES = {}
for _n, _offset in enumerate(OFFSETS):
    for _axis, _step, _classes in routes(_offset):
        EDGES[(_n, _axis, _step)] = len(EDGES)


def wrap(value):
    return lax.rem(value, RING)


def kernel(
    blk_ref, pos_ref, permt_ref, load_ref, thick_ref, delay_ref, out_ref,
    buf, meta, wraw, wperm, wt, onehot, rows_id, sel, shifted, acc, part, arrived,
    edge_sem, recv_sem, relay_send, relay_recv, meta_send, meta_recv, w_sem, own_sem, rs_send, rs_recv,
):
    p = lax.axis_index("panel")
    o = lax.axis_index("obs")
    x_lo, core = p // 2, lax.rem(p, 2)
    y, z, x_hi = o // 8, lax.rem(o // 2, 4), lax.rem(o, 2)
    x = x_hi * 2 + x_lo
    me = (x, y, z)

    def device(cx, cy, cz, cc):
        return (lax.rem(cx, 2) * 2 + cc, cy * 8 + cz * 2 + cx // 2)

    def beside(axis, step):
        there = list(me)
        there[axis] = wrap(me[axis] + step)
        return device(*there, core)

    near = {(axis, step): beside(axis, step) for axis in range(3) for step in (1, 3)}
    partner = device(x, y, z, 1 - core)
    line = [(device(wrap(x + s), y, z, core), s * 2) for s in range(1, 4)]
    line += [(device(wrap(x + s), y, z, 1 - core), s * 2 + 1) for s in range(0, 4)]
    column = [(device(x, y, wrap(z + s), core), s) for s in range(1, 4)]
    plane = [(device(x, wrap(y + s), z, core), s) for s in range(1, 4)]

    for index, source in enumerate((load_ref, thick_ref)):
        pltpu.make_async_copy(source, wraw.at[index], w_sem.at[index]).start()
    own = pltpu.make_async_copy(blk_ref, buf.at[0, 0], own_sem.at[0])
    own.start()
    own_meta = pltpu.make_async_copy(pos_ref, meta.at[y, z, x * 2 + core], own_sem.at[1])
    own_meta.start()

    barrier = pltpu.get_barrier_semaphore()
    for target, unused in line + column + plane:
        pl.semaphore_signal(barrier, inc=1, device_id=target, device_id_type=MESH)
    pl.semaphore_wait(barrier, 13)

    def source_of(n):
        offset = OFFSETS[n]
        return [wrap(me[i] + (RING - offset[i])) for i in range(3)]

    def edges(n, act):
        offset = OFFSETS[n]
        there = source_of(n)
        kind = lax.rem(there[0] + there[1] + there[2] + core, 3)
        for axis, step, classes in routes(offset):
            landed = list(offset)
            landed[axis] = (offset[axis] + step) % RING
            slot = PLACE[tuple(landed)]
            edge = EDGES[(n, axis, step)]
            copy = pltpu.make_async_remote_copy(
                src_ref=blk_ref if n == 0 else buf.at[0, n],
                dst_ref=buf.at[0, slot],
                send_sem=edge_sem.at[edge],
                recv_sem=recv_sem.at[slot],
                device_id=near[(axis, step)],
                device_id_type=MESH,
            )
            if len(classes) == 3:
                act(copy)
            else:
                test = kind == classes[0]
                for k in classes[1:]:
                    test = jnp.logical_or(test, kind == k)

                @pl.when(test)
                def _():
                    act(copy)

    def arrival(n):
        return pltpu.make_async_remote_copy(
            src_ref=blk_ref, dst_ref=buf.at[0, n], send_sem=edge_sem.at[0], recv_sem=recv_sem.at[n],
            device_id=partner, device_id_type=MESH,
        )

    def relay(group):
        span = pl.ds(group * RELAY, RELAY)
        return pltpu.make_async_remote_copy(
            src_ref=buf.at[0, span], dst_ref=buf.at[1, span],
            send_sem=relay_send.at[group], recv_sem=relay_recv.at[group],
            device_id=partner, device_id_type=MESH,
        )

    def meta_copy(ref, ref_there, number, target):
        return pltpu.make_async_remote_copy(
            src_ref=ref, dst_ref=ref_there, send_sem=meta_send.at[number], recv_sem=meta_recv.at[number],
            device_id=target, device_id_type=MESH,
        )

    mine = meta.at[y, z, x * 2 + core]
    stages = [
        [meta_copy(pos_ref, mine, number, target) for number, (target, unused) in enumerate(line)],
        [meta_copy(meta.at[y, z], meta.at[y, z], 7 + i, t) for i, (t, unused) in enumerate(column)],
        [meta_copy(meta.at[y], meta.at[y], 10 + i, t) for i, (t, unused) in enumerate(plane)],
    ]

    edges(0, lambda copy: copy.start())
    for copy in stages[0]:
        copy.start()
    own.wait()
    own_meta.wait()

    rows_id[...] = (lax.broadcasted_iota(jnp.int32, (512, 128), 0) - 256).astype(jnp.float32).astype(jnp.bfloat16)
    acc[...] = jnp.zeros_like(acc)
    for index, source in enumerate((load_ref, thick_ref)):
        pltpu.make_async_copy(source, wraw.at[index], w_sem.at[index]).wait()

    def order_weights(first, last):
        @pl.loop(first, last)
        def _(d):
            span = pl.ds(pl.multiple_of(d * 256, 256), 256)
            both = jnp.concatenate([wraw[0, span, :], wraw[1, span, :]], axis=1)
            moved = jnp.dot(permt_ref[...], both, preferred_element_type=jnp.float32).astype(jnp.bfloat16)
            place = pl.ds(pl.multiple_of(d * 16, 16), 16)
            for g in range(2 * CHUNKS):
                wperm[g, 0, place, :] = moved[g * 16 : (g + 1) * 16, :128]
                wperm[g, 1, place, :] = moved[g * 16 : (g + 1) * 16, 128:]

    def turn_weights(first, last):
        @pl.loop(first, last)
        def _(g):
            for index in range(2):
                wt[g, :, index * 512 : (index + 1) * 512] = wperm[g, index].T

    lane = lax.broadcasted_iota(jnp.int32, (32, 128), 1)

    def chunk(m, side):
        for i in range(CHUNK):
            sx, sy, sz = source_of(m * CHUNK + i)
            source_core = core if side == 0 else 1 - core
            pos = meta[sy, sz, sx * 2 + source_core]
            q = pos - 64.0 * p.astype(jnp.float32)
            inside = jnp.logical_and(q > -0.5, q < 63.5)
            target = jnp.where(inside, q * 8.0 + (i - 256.0), 1000.0).astype(jnp.bfloat16)
            onehot[:, i * 128 : (i + 1) * 128] = jnp.where(
                rows_id[...] == target, jnp.ones((), jnp.bfloat16), jnp.zeros((), jnp.bfloat16)
            )
        raw = buf[side, m * CHUNK : (m + 1) * CHUNK].reshape(CHUNK * 128, 256)
        sel[...] = jnp.dot(onehot[...], raw, preferred_element_type=jnp.float32)
        for b in range(16):
            delay = delay_ref[b, 0]
            keep = lane >= delay
            for index in range(2):
                piece = sel[b * 32 : (b + 1) * 32, index * 128 : (index + 1) * 128]
                piece = jnp.where(keep, pltpu.roll(piece, delay, 1), 0.0)
                shifted[index * 512 + b * 32 : index * 512 + (b + 1) * 32, :] = piece.astype(jnp.bfloat16)
        acc[...] += jnp.dot(wt[side * CHUNKS + m], shifted[...], preferred_element_type=jnp.float32)

    order_weights(0, 16)
    pending = []
    done_relays = set()

    def work(item):
        m, side = item
        if side == 1:
            for group in range(m * CHUNK // RELAY, (m + 1) * CHUNK // RELAY):
                relay(group).wait_recv()
        chunk(m, side)

    for n in range(1, CHIPS):
        arrival(n).wait_recv()
        edges(n, lambda copy: copy.start())
        if n % RELAY == RELAY - 1:
            relay(n // RELAY).start()
        if n == 6:
            for copy in stages[0]:
                copy.wait_recv()
            for copy in stages[1]:
                copy.start()
            order_weights(16, 32)
        if n == 21:
            for copy in stages[1]:
                copy.wait_recv()
            for copy in stages[2]:
                copy.start()
        if n in (12, 16):
            turn_weights(0 if n == 12 else 8, 8 if n == 12 else 16)
        if n % CHUNK == CHUNK - 1:
            pending.append((n // CHUNK, 0))
            if n // CHUNK > 0:
                pending.append((n // CHUNK - 1, 1))
        if n == 31:
            for copy in stages[2]:
                copy.wait_recv()
        if n >= 32 and n % 3 == 0 and pending:
            work(pending.pop(0))
    pending.append((CHUNKS - 1, 1))
    for item in pending:
        work(item)

    part[...] = acc[...].T
    shares = []
    for step in range(1, 4):
        there = lax.rem(p + step, 4)
        shares.append(
            pltpu.make_async_remote_copy(
                src_ref=part.at[pl.ds(pl.multiple_of(there * 32, 32), 32), :],
                dst_ref=arrived.at[step - 1],
                send_sem=rs_send.at[step - 1],
                recv_sem=rs_recv.at[step - 1],
                device_id=(there, o),
                device_id_type=MESH,
            )
        )
    for copy in shares:
        copy.start()
    total = part[pl.ds(pl.multiple_of(p * 32, 32), 32), :]
    for n in range(CHIPS):
        edges(n, lambda copy: copy.wait_send())
    for group in range(CHIPS // RELAY):
        relay(group).wait_send()
    for stage in stages:
        for copy in stage:
            copy.wait_send()
    for copy in shares:
        copy.wait()
    out_ref[...] = total + arrived[0] + arrived[1] + arrived[2]


def per_device(les_rows, les_dest, loading_weight, thickness_weight, delays):
    p = lax.axis_index("panel")
    o = lax.axis_index("obs")
    velocity = jnp.pad(les_rows[:, 1, :].astype(jnp.float32), ((0, 0), (1, 1)))
    rate = ((velocity[:, 2:] - velocity[:, :-2]) * 0.5).astype(jnp.bfloat16)
    blk = jnp.concatenate([les_rows[:, 0, :], rate], axis=1)
    dest = les_dest[:, 0]
    row = jnp.arange(dest.shape[0], dtype=jnp.int32)
    same = jnp.logical_and(dest[:, None] == dest[None, :], row[:, None] < row[None, :])
    rank = jnp.sum(same.astype(jnp.int32), axis=0)
    pos = (dest * 2 + rank).astype(jnp.float32).reshape(1, -1)

    x = lax.rem(o, 2) * 2 + p // 2
    core = lax.rem(p, 2)
    index = np.arange(256)
    side, m, cap, i = index // 128, index // 16 % 8, index // 8 % 2, index % 8
    offsets = np.array(OFFSETS)[m * CHUNK + i]
    sx = lax.rem(x + jnp.asarray(4 - offsets[:, 0], jnp.int32), 4)
    sy = lax.rem(o // 8 + jnp.asarray(4 - offsets[:, 1], jnp.int32), 4)
    sz = lax.rem(lax.rem(o // 2, 4) + jnp.asarray(4 - offsets[:, 2], jnp.int32), 4)
    sc = lax.rem(core + jnp.asarray(side, jnp.int32), 2)
    owner = (lax.rem(sx, 2) * 2 + sc) * 32 + sy * 8 + sz * 2 + sx // 2
    want = owner * 2 + jnp.asarray(cap, jnp.int32)
    permt = (want[:, None] == jnp.arange(256, dtype=jnp.int32)[None, :]).astype(jnp.bfloat16)

    vmem = pl.BlockSpec(memory_space=pltpu.VMEM)
    return pl.pallas_call(
        kernel,
        out_shape=jax.ShapeDtypeStruct((32, 128), jnp.float32),
        in_specs=[vmem, vmem, vmem, pl.BlockSpec(memory_space=pl.ANY), pl.BlockSpec(memory_space=pl.ANY),
                  pl.BlockSpec(memory_space=pltpu.SMEM)],
        out_specs=vmem,
        scratch_shapes=[
            pltpu.VMEM((2, CHIPS, 128, 256), jnp.bfloat16),
            pltpu.VMEM((4, 4, 8, 1, 128), jnp.float32),
            pltpu.VMEM((2, 8192, 128), jnp.bfloat16),
            pltpu.VMEM((2 * CHUNKS, 2, 512, 128), jnp.bfloat16),
            pltpu.VMEM((2 * CHUNKS, 128, 1024), jnp.bfloat16),
            pltpu.VMEM((512, 1024), jnp.bfloat16),
            pltpu.VMEM((512, 128), jnp.bfloat16),
            pltpu.VMEM((512, 256), jnp.float32),
            pltpu.VMEM((1024, 128), jnp.bfloat16),
            pltpu.VMEM((128, 128), jnp.float32),
            pltpu.VMEM((128, 128), jnp.float32),
            pltpu.VMEM((3, 32, 128), jnp.float32),
            pltpu.SemaphoreType.DMA((len(EDGES),)),
            pltpu.SemaphoreType.DMA((CHIPS,)),
            pltpu.SemaphoreType.DMA((CHIPS // RELAY,)),
            pltpu.SemaphoreType.DMA((CHIPS // RELAY,)),
            pltpu.SemaphoreType.DMA((13,)),
            pltpu.SemaphoreType.DMA((13,)),
            pltpu.SemaphoreType.DMA((2,)),
            pltpu.SemaphoreType.DMA((2,)),
            pltpu.SemaphoreType.DMA((3,)),
            pltpu.SemaphoreType.DMA((3,)),
        ],
        compiler_params=pltpu.CompilerParams(collective_id=0, has_side_effects=True, vmem_limit_bytes=48 << 20),
    )(blk, pos, permt, loading_weight, thickness_weight, delays)


def solution(mesh):
    placed = (
        P(("panel", "obs"), None, None),
        P(("panel", "obs"), None),
        P("panel", "obs"),
        P("panel", "obs"),
        P("panel", "obs"),
    )
    return jax.shard_map(
        per_device, mesh=mesh, in_specs=placed, out_specs=P("panel", "obs"), check_vma=False
    )
```

time: 226 us -> 61.2 us (0.27)
  waiting for transfers between devices: 92.7 us -> 0 us
  Pallas kernels: 0 us -> 52.5 us
  matrix products: 37.2 us -> 0 us
  loops' own time: 28.7 us -> 0 us
  blocking collectives: 21.3 us -> 0 us
  other arithmetic: 16 us -> 2.53 us
  between operations: 13.5 us -> 0.05 us
  local copies, waits for them, and re-layouts: 14.9 us -> 5.57 us
    all_gather x1 -> x0, waiting for transfers between devices: 75.2 us -> none  [per_device(): group = lax.all_gather(local, 'obs', axis=0, tiled=True)]
    pallas_call x0 -> x1, Pallas kernels: none -> 52.5 us  [per_device(): pl.pallas_call(kernel, out_shape=jax.ShapeDtypeStruct((32, 128), jnp.floa...]
    dot_general x32 -> x0, matrix products: 37.2 us -> none  [the longest x16 19.1 us: one_block(): lax.dot_general(press_b, load_b, dims, preferred_element_type=jnp.float32)]
    another operation x1 -> x0, loops' own time: 28.7 us -> none  [per_device(): lax.scan(one_block, start, (press_blocks, rate_blocks, load_blocks, thick...]
    all_to_all x1 -> x0, blocking collectives: 21.3 us -> none  [per_device(): lax.all_to_all(buffer.reshape(count, cap, 2, steps), ('panel', 'obs'), sp...]
    reduce_scatter x1 -> x0, waiting for transfers between devices: 17.5 us -> none  [per_device(): lax.psum_scatter(partial_sum, 'panel', scatter_dimension=0, tiled=True)]
    sub x16 -> x0, other arithmetic: 10.4 us -> none  [delay_block(): start = steps - delay]
    scatter x1 -> x0, local copies, waits for them, and re-layouts: 9.74 us -> none  [per_device(): jnp.zeros((count * cap, 2, steps), les_rows.dtype).at[position]]
  transfers between devices with their start and end apart: 2 -> 0, of which waited for: 2 -> 0; matrix products, arithmetic and copies ran while one was open for 0% -> 0% of each run, Pallas kernels for 0% -> 0%
where the time goes in v1:
time: 61.2 us; the launch traced here: 60.6 us
  Pallas kernels  52.5 us (86%)
  local copies, waits for them, and re-layouts  5.57 us (9%)
  other arithmetic  2.53 us (4%)
    pallas_call x1, Pallas kernels, per_device(): pl.pallas_call(kernel, out_shape=jax.ShapeDtypeStruct((32, 128), jnp.floa...  52.5 us
    unnamed x6, local copies, waits for them, and re-layouts  4.52 us

profile of v1, /device:TPU:1, one launch (start us, length us, event | category | flops | bytes accessed | tf_op | source)
XLA Modules:
  0.0 60.6 jit_solution(2125089461498573381)
XLA Ops:
  0.0 1.0 %fusion.16 = (bf16[128,1,128]{2,1,0:T(2,128)(2,1)S(1)}, bf16[128,1,128]{2,1,0:T(2,128)(2,1)S(1)}) fusion(bf16[128,2,128]{2,1,0:T(2,128)(2,1)} %param.10), kind=kLoop, calls=%fused_computation.42 | loop fusion | bytes 131072 | tf_op jit(solution)/shard_map/slice | solution.py:278
  1.1 0.1 pad_convert_fusion
  1.1 0.1 fusion.2
  1.3 0.8 %convert_reduce_fusion = s32[128]{0:T(128)S(1)} fusion(s32[128]{0:T(128)} %bitcast.11), kind=kLoop, calls=%fused_computation.6 | loop fusion | flops 81792 | bytes 1024 | tf_op jit(solution)/shard_map/reduce_sum | solution.py:282
  2.1 0.7 %fusion.15.pos_ref = f32[1,128]{1,0:T(1,128)S(1)} fusion(s32[128]{0:T(128)S(1)} %convert_reduce_fusion, s32[128,1]{0,1:T(1,128)} %param.11), kind=kLoop, calls=%fused_computation.41 | loop fusion | flops 384 | bytes 1536 | tf_op jit(solution)/shard_map/convert_element_type | solution.py:283
  2.7 0.8 %multiply_add_fusion = s32[256]{0:T(256)S(1)} fusion(s32[256]{0:T(256)} %constant.89.clone, s32[256]{0:T(256)} %constant.87.clone, s32[256]{0:T(256)} %constant.86.clone, s32[256]{0:T(256)} %constant.88.clone, s32[256]{0:T(256)} %constant.85.clone, s32[]{:T(128)S(6)} %rem.168, s32[]{:T(128)S(6)} %select_n.17, s32[]{:T(128)S(6)} %rem.133, s32[]{:T(128)S(6)} %add.59), kind=kLoop, calls=%fused_computation.39 | loop fusion | flops 13568 | bytes 6160 | tf_op jit(solution)/shard_map/add | solution.py:295
  3.5 0.1 fusion.permt_ref
  3.6 0.7 %copy.16.delay_ref = s32[16,1]{1,0:T(8,128)S(1)} copy(s32[16,1]{0,1:T(1,128)} %param.14) | data formatting | bytes 128 | tf_op args[4]
  4.4 0.0 copy-start
  4.4 1.6 %copy-done = bf16[8192,128]{1,0:T(8,128)(2,1)S(1)} copy-done((bf16[8192,128]{1,0:T(8,128)(2,1)S(1)}, bf16[8192,128]{1,0:T(8,128)(2,1)}, u32[]{:S(2)}) %copy-start) | copy-done | bytes 2097176
  5.9 0.0 copy-start.1
  5.9 1.6 %copy-done.1 = bf16[8192,128]{1,0:T(8,128)(2,1)S(1)} copy-done((bf16[8192,128]{1,0:T(8,128)(2,1)S(1)}, bf16[8192,128]{1,0:T(8,128)(2,1)}, u32[]{:S(2)}) %copy-start.1) | copy-done | bytes 2097176
  7.5 52.5 %shard_map.100 = f32[32,128]{1,0:T(8,128)S(1)} custom-call(bf16[128,256]{1,0:T(8,128)(2,1)S(1)} %pad_maximum_fusion.blk_ref, f32[1,128]{1,0:T(1,128)S(1)} %fusion.15.pos_ref, bf16[256,256]{1,0:T(8,128)(2,1)S(1)} %fusion.permt_ref, bf16[8192,128]{1,0:T(8,128)(2,1)S(1)} %copy-done, bf16[8192,128]{1,0:T(8,128)(2,1)S(1)} %copy-done.1, s32[16,1]{1,0:T(8,128)S(1)} %copy.16.delay_ref), custom_call_target="tpu_custom_call" | custom-call | tf_op jit(solution)/shard_map/pallas_call | solution.py:299
  60.0 0.6 %copy.22 = f32[32,128]{1,0:T(8,128)} copy(f32[32,128]{1,0:T(8,128)S(1)} %shard_map.100) | data formatting | bytes 32768
  (2 shorter events, 0.0 us)
Async XLA Ops:
  4.4 1.6 %copy-start = (bf16[8192,128]{1,0:T(8,128)(2,1)S(1)}, bf16[8192,128]{1,0:T(8,128)(2,1)}, u32[]{:S(2)}) copy-start(bf16[8192,128]{1,0:T(8,128)(2,1)} %load_ref.1) | copy-start | bytes 6291460
  5.9 1.6 %copy-start.1 = (bf16[8192,128]{1,0:T(8,128)(2,1)S(1)}, bf16[8192,128]{1,0:T(8,128)(2,1)}, u32[]{:S(2)}) copy-start(bf16[8192,128]{1,0:T(8,128)(2,1)} %thick_ref.1) | copy-start | bytes 6291460

commit v2 on v0

v2 whole, which is shorter than its diff:
```python
import itertools

import jax
import jax.numpy as jnp
import numpy as np
from jax import lax
from jax.experimental import pallas as pl
from jax.experimental.pallas import tpu as pltpu
from jax.sharding import PartitionSpec as P

MESH = pl.DeviceIdType.MESH
RING = 4
CHIPS = RING**3
CHUNK = 4
CHUNKS = CHIPS // CHUNK
ROWS = (48, 48, 32)
FIRST = (0, 48, 96)

STAGE1 = [(h, 0, 0, s) for s in (1, 3, 2) for h in range(3)]
STAGE2 = [(h, 0, s, None) for s in (1, 3, 2) for h in range(3)]
STAGE3 = [(h, s, g, None) for g, s in (
    (0, 1), (0, 3), (0, 2), (1, 1), (1, 3), (3, 1), (3, 3), (2, 1), (2, 3), (1, 2), (3, 2), (2, 2),
) for h in range(3)]
ARRIVALS = STAGE1 + STAGE2[:6] + STAGE3[:6] + STAGE2[6:] + STAGE3[6:]
NUMBER = {item: i for i, item in enumerate(ARRIVALS)}
GROUPS = [(h, 0, 0, None) for h in range(3)] + ARRIVALS[9:]
GROUP = {item: i for i, item in enumerate(GROUPS)}


def copies_after(item):
    h, o3, o2, o1 = item
    second, third = (h + 1) % 3, (h + 2) % 3
    if o1 is not None:
        return []
    if o3 == 0:
        found = [((h, 0, s, None), second, s) for s in (1, 3, 2)] if o2 == 0 else []
        return found + [((h, s, o2, None), third, s) for s in (1, 3)]
    turn = 1 if o2 % 2 == 0 else 3
    return [((h, 2, o2, None), third, turn)] if o3 == turn else []


def group_of(offset, h):
    return (h, offset[(h + 2) % 3], offset[(h + 1) % 3], None)


OFFSETS = sorted(
    itertools.product(range(RING), repeat=3), key=lambda o: (max(GROUP[group_of(o, h)] for h in range(3)), o)
)
READY = [max(GROUP[group_of(o, h)] for o in OFFSETS[m * CHUNK : (m + 1) * CHUNK] for h in range(3)) for m in range(CHUNKS)]


def kernel(
    blk_ref, code_ref, dest_ref, load_ref, thick_ref, delay_ref, out_ref,
    buf0, buf1, buf2, meta, pos, codes, dest, delays, permt, wraw, wperm, wt, onehot, sel, shifted, acc, part, arrived,
    own_sem, send1, recv1, relay_send, relay_recv, meta_send, meta_recv, rs_send, rs_recv,
):
    bufs = (buf0, buf1, buf2)
    p = lax.axis_index("panel")
    o = lax.axis_index("obs")
    x_lo, core = p // 2, lax.rem(p, 2)
    y, z, x_hi = o // 8, lax.rem(o // 2, 4), lax.rem(o, 2)
    x = x_hi * 2 + x_lo

    def device(cx, cy, cz, cc):
        return (lax.rem(cx, 2) * 2 + cc, cy * 8 + cz * 2 + cx // 2)

    line = [device(lax.rem(x + s, RING), y, z, core) for s in range(1, 4)]
    line += [device(lax.rem(x + s, RING), y, z, 1 - core) for s in range(0, 4)]
    column = [device(x, y, lax.rem(z + s, RING), core) for s in range(1, 4)]
    plane = [device(x, lax.rem(y + s, RING), z, core) for s in range(1, 4)]
    partner = line[3]
    first = core == 0

    def pick(a, b):
        return tuple(jnp.where(first, u, v) for u, v in zip(a, b))

    near = {}
    for s in range(1, 4):
        near[(0, s)] = pick(line[s - 1], plane[s - 1])
        near[(1, s)] = pick(plane[s - 1], column[s - 1])
        near[(2, s)] = pick(column[s - 1], line[s - 1])

    turned = ((x, y, z), (y, z, x))
    back = []
    for side in range(2):
        mine = pick(turned[side], turned[1 - side])
        back.append([[lax.rem(mine[i] + (RING - v), RING) for v in range(RING)] for i in range(3)])

    local = [
        pltpu.make_async_copy(load_ref, wraw.at[0], own_sem.at[0]),
        pltpu.make_async_copy(thick_ref, wraw.at[1], own_sem.at[1]),
        pltpu.make_async_copy(code_ref, codes, own_sem.at[2]),
        pltpu.make_async_copy(dest_ref, dest, own_sem.at[3]),
        pltpu.make_async_copy(delay_ref, delays, own_sem.at[4]),
    ]
    for copy in (local[3], local[2], local[0], local[1], local[4]):
        copy.start()
    own = [
        pltpu.make_async_copy(blk_ref.at[pl.ds(FIRST[h], ROWS[h])], bufs[h].at[0, 0], own_sem.at[5 + h]) for h in range(3)
    ]
    for copy in own:
        copy.start()

    barrier = pltpu.get_barrier_semaphore()
    for target in line + column + plane:
        pl.semaphore_signal(barrier, inc=1, device_id=target, device_id_type=MESH)
    pl.semaphore_wait(barrier, 13)

    def span(item):
        h, o3, o2, o1 = item
        at = (o3 * RING + o2) * RING
        return bufs[h], (pl.ds(at, RING) if o1 is None else at + o1)

    def remote(source, item, target):
        ref, where = span(item)
        return pltpu.make_async_remote_copy(
            src_ref=source, dst_ref=ref.at[0, where], send_sem=send1.at[NUMBER[item]], recv_sem=recv1.at[NUMBER[item]],
            device_id=target, device_id_type=MESH,
        )

    def arrival(item):
        ref, where = span(item)
        return remote(ref.at[0, where], item, partner)

    sent = []

    def send(source, item, axis, step):
        copy = remote(source, item, near[(axis, step)])
        copy.start()
        sent.append(copy)

    def forward(item):
        ref, where = span(item)
        for landed, axis, step in copies_after(item):
            send(ref.at[0, where], landed, axis, step)
        relay(item).start()

    def relay(item):
        ref, where = span(item)
        return pltpu.make_async_remote_copy(
            src_ref=ref.at[0, where], dst_ref=ref.at[1, where],
            send_sem=relay_send.at[GROUP[item]], recv_sem=relay_recv.at[GROUP[item]],
            device_id=partner, device_id_type=MESH,
        )

    for s in (1, 3, 2):
        for h in range(3):
            send(blk_ref.at[pl.ds(FIRST[h], ROWS[h])], (h, 0, 0, s), h, s)

    local[3].wait()
    here = jnp.broadcast_to(dest[...], (128, 128)).astype(jnp.float32)
    there = here.T
    earlier = lax.broadcasted_iota(jnp.int32, (128, 128), 0) < lax.broadcasted_iota(jnp.int32, (128, 128), 1)
    same = jnp.where(jnp.logical_and(here == there, earlier), 1.0, 0.0)
    pos[...] = there[0:1, :] * 2.0 + jnp.sum(same, axis=0, keepdims=True)

    local[2].wait()
    for side in range(2):
        code = codes[side * 128 : (side + 1) * 128, :]
        along = []
        for i in range(3):
            digit = lax.rem(code // (RING**i), RING)
            value = jnp.zeros_like(digit)
            for v in range(RING):
                value = jnp.where(digit == v, back[side][i][v], value)
            along.append(value)
        straight = first if side == 0 else jnp.logical_not(first)
        sx, sy, sz = (jnp.where(straight, along[a], along[b]) for a, b in ((0, 2), (1, 0), (2, 1)))
        source_core = core if side == 0 else 1 - core
        owner = (lax.rem(sx, 2) * 2 + source_core) * 32 + sy * 8 + sz * 2 + sx // 2
        want = owner * 2 + code // CHIPS
        for half in range(2):
            column_id = lax.broadcasted_iota(jnp.int32, (128, 128), 1) + half * 128
            permt[side * 128 : (side + 1) * 128, half * 128 : (half + 1) * 128] = jnp.where(
                want == column_id, 1.0, 0.0
            ).astype(jnp.bfloat16)

    own_meta = pltpu.make_async_copy(pos, meta.at[y * 32 + z * 8 + x * 2 + core], own_sem.at[8])
    own_meta.start()
    for copy in own:
        copy.wait()
    for index in range(2):
        local[index].wait()

    def order_weights(start, stop):
        @pl.loop(start, stop)
        def _(d):
            rows = pl.ds(pl.multiple_of(d * 256, 256), 256)
            both = jnp.concatenate([wraw[0, rows, :], wraw[1, rows, :]], axis=1)
            moved = jnp.dot(permt[...], both, preferred_element_type=jnp.float32)
            place = pl.ds(pl.multiple_of(d * 8, 8), 8)
            for g in range(2 * CHUNKS):
                wperm[g, 0, place, :] = moved[g * 8 : (g + 1) * 8, :128]
                wperm[g, 1, place, :] = moved[g * 8 : (g + 1) * 8, 128:]

    def turn_weights(start, stop):
        @pl.loop(start, stop)
        def _(g):
            for index in range(2):
                wt[g, :, index * 256 : (index + 1) * 256] = wperm[g, index].astype(jnp.bfloat16).T

    lane = lax.broadcasted_iota(jnp.int32, (16, 128), 1)
    row_id = lax.broadcasted_iota(jnp.int32, (256, 128), 0).astype(jnp.float32).astype(jnp.bfloat16)
    group_first = 64.0 * p.astype(jnp.float32)
    one, nil = jnp.ones((), jnp.bfloat16), jnp.zeros((), jnp.bfloat16)
    weights = ((2, 32, 8), (32, 8, 2))
    index_of = []
    for side in range(2):
        scale = pick(weights[side], weights[1 - side])
        source_core = core if side == 0 else 1 - core
        index_of.append(
            [[back[side][i][v] * scale[i] + (source_core if i == 0 else 0) for v in range(RING)] for i in range(3)]
        )

    def chunk(m, side):
        pieces = []
        for i in range(CHUNK):
            offset = OFFSETS[m * CHUNK + i]
            tab = index_of[side]
            q = meta[tab[0][offset[0]] + tab[1][offset[1]] + tab[2][offset[2]]] - group_first
            inside = jnp.logical_and(q > -0.5, q < 63.5)
            target = jnp.where(inside, q * float(CHUNK) + float(i), 1000.0).astype(jnp.bfloat16)
            onehot[:, i * 128 : (i + 1) * 128] = jnp.where(row_id == target, one, nil)
            for h in range(3):
                unused, o3, o2, unused = group_of(offset, h)
                pieces.append(bufs[h][side, (o3 * RING + o2) * RING + offset[h]])
        raw = jnp.concatenate(pieces, axis=0)
        sel[...] = jnp.dot(onehot[...], raw, preferred_element_type=jnp.float32)
        for b in range(16):
            delay = delays[b, 0]
            keep = lane >= delay
            for index in range(2):
                piece = sel[b * 16 : (b + 1) * 16, index * 128 : (index + 1) * 128]
                piece = jnp.where(keep, pltpu.roll(piece, delay, 1), 0.0)
                shifted[index * 256 + b * 16 : index * 256 + (b + 1) * 16, :] = piece.astype(jnp.bfloat16)
        acc[...] += jnp.dot(wt[side * CHUNKS + m], shifted[...], preferred_element_type=jnp.float32)

    def meta_copy(ref, ref_there, number, target):
        return pltpu.make_async_remote_copy(
            src_ref=ref, dst_ref=ref_there, send_sem=meta_send.at[number], recv_sem=meta_recv.at[number],
            device_id=target, device_id_type=MESH,
        )

    mine = meta.at[y * 32 + z * 8 + x * 2 + core]
    ring_z = meta.at[pl.ds(y * 32 + z * 8, 8)]
    ring_y = meta.at[pl.ds(y * 32, 32)]
    stages = [
        [meta_copy(pos, mine, number, target) for number, target in enumerate(line)],
        [meta_copy(ring_z, ring_z, 7 + i, target) for i, target in enumerate(column)],
        [meta_copy(ring_y, ring_y, 10 + i, target) for i, target in enumerate(plane)],
    ]

    acc[...] = jnp.zeros_like(acc)
    order_weights(0, 4)
    own_meta.wait()
    for copy in stages[0]:
        copy.start()
    order_weights(4, 8)
    local[4].wait()

    todo = []
    relayed = set()

    def work(item):
        unused, m, side = item
        if side == 1:
            needed = sorted({GROUP[group_of(offset, h)] for offset in OFFSETS[m * CHUNK : (m + 1) * CHUNK] for h in range(3)})
            for g in needed:
                if g not in relayed:
                    relayed.add(g)
                    relay(GROUPS[g]).wait_recv()
        chunk(m, side)

    for item in STAGE1:
        arrival(item).wait_recv()
    for h in range(3):
        forward((h, 0, 0, None))
    for copy in stages[0]:
        copy.wait_recv()
    for copy in stages[1]:
        copy.start()
    order_weights(8, 28)
    for copy in stages[1]:
        copy.wait_recv()
    for copy in stages[2]:
        copy.start()
    late = len(GROUPS)
    for m in range(CHUNKS):
        todo.append((READY[m], m, 0))
        todo.append((READY[m] + LAG, m, 1))
    todo.sort()
    for item in ARRIVALS[9:]:
        arrival(item).wait_recv()
        forward(item)
        now = GROUP[item]
        if item == STAGE2[5]:
            order_weights(28, 32)
            turn_weights(0, 8)
        if item == STAGE3[5]:
            turn_weights(8, 32)
            for copy in stages[2]:
                copy.wait_recv()
        if now >= GROUP[STAGE3[5]]:
            for unused in range(2):
                if todo and todo[0][0] <= now:
                    work(todo.pop(0))
    for item in todo:
        work(item)

    part[...] = acc[...].T
    shares = []
    for step in range(1, 4):
        place = lax.rem(p + step, 4)
        shares.append(
            pltpu.make_async_remote_copy(
                src_ref=part.at[pl.ds(pl.multiple_of(place * 32, 32), 32), :],
                dst_ref=arrived.at[step - 1],
                send_sem=rs_send.at[step - 1],
                recv_sem=rs_recv.at[step - 1],
                device_id=(place, o),
                device_id_type=MESH,
            )
        )
    for copy in shares:
        copy.start()
    total = part[pl.ds(pl.multiple_of(p * 32, 32), 32), :]
    for copy in sent:
        copy.wait_send()
    for item in GROUPS:
        relay(item).wait_send()
    for stage in stages:
        for copy in stage:
            copy.wait_send()
    for copy in shares:
        copy.wait()
    out_ref[...] = total + arrived[0] + arrived[1] + arrived[2]


LAG = 4


def per_device(les_rows, les_dest, loading_weight, thickness_weight, delays):
    velocity = jnp.pad(les_rows[:, 1, :].astype(jnp.float32), ((0, 0), (1, 1)))
    rate = ((velocity[:, 2:] - velocity[:, :-2]) * 0.5).astype(jnp.bfloat16)
    blk = jnp.concatenate([les_rows[:, 0, :], rate], axis=1)

    index = np.arange(256)
    m, cap, i = index // 8 % CHUNKS, index // CHUNK % 2, index % CHUNK
    offsets = np.array(OFFSETS)[m * CHUNK + i]
    code = offsets @ np.array([1, RING, RING**2]) + CHIPS * cap
    code = jnp.asarray(np.repeat(code[:, None], 128, axis=1), jnp.int32)

    vmem = pl.BlockSpec(memory_space=pltpu.VMEM)
    hbm = pl.BlockSpec(memory_space=pltpu.HBM)
    return pl.pallas_call(
        kernel,
        out_shape=jax.ShapeDtypeStruct((32, 128), jnp.float32),
        in_specs=[vmem, hbm, hbm, hbm, hbm, hbm],
        out_specs=vmem,
        scratch_shapes=[
            pltpu.VMEM((2, CHIPS, ROWS[0], 256), jnp.bfloat16),
            pltpu.VMEM((2, CHIPS, ROWS[1], 256), jnp.bfloat16),
            pltpu.VMEM((2, CHIPS, ROWS[2], 256), jnp.bfloat16),
            pltpu.VMEM((128, 1, 128), jnp.float32),
            pltpu.VMEM((1, 128), jnp.float32),
            pltpu.VMEM((256, 128), jnp.int32),
            pltpu.VMEM((128, 1), jnp.int32),
            pltpu.SMEM((16, 1), jnp.int32),
            pltpu.VMEM((256, 256), jnp.bfloat16),
            pltpu.VMEM((2, 8192, 128), jnp.bfloat16),
            pltpu.VMEM((2 * CHUNKS, 2, 256, 128), jnp.float32),
            pltpu.VMEM((2 * CHUNKS, 128, 512), jnp.bfloat16),
            pltpu.VMEM((256, 512), jnp.bfloat16),
            pltpu.VMEM((256, 256), jnp.float32),
            pltpu.VMEM((512, 128), jnp.bfloat16),
            pltpu.VMEM((128, 128), jnp.float32),
            pltpu.VMEM((128, 128), jnp.float32),
            pltpu.VMEM((3, 32, 128), jnp.float32),
            pltpu.SemaphoreType.DMA((9,)),
            pltpu.SemaphoreType.DMA((len(ARRIVALS),)),
            pltpu.SemaphoreType.DMA((len(ARRIVALS),)),
            pltpu.SemaphoreType.DMA((len(GROUPS),)),
            pltpu.SemaphoreType.DMA((len(GROUPS),)),
            pltpu.SemaphoreType.DMA((13,)),
            pltpu.SemaphoreType.DMA((13,)),
            pltpu.SemaphoreType.DMA((3,)),
            pltpu.SemaphoreType.DMA((3,)),
        ],
        compiler_params=pltpu.CompilerParams(collective_id=0, has_side_effects=True, vmem_limit_bytes=60 << 20),
    )(blk, code, les_dest, loading_weight, thickness_weight, delays)


def solution(mesh):
    placed = (
        P(("panel", "obs"), None, None),
        P(("panel", "obs"), None),
        P("panel", "obs"),
        P("panel", "obs"),
        P("panel", "obs"),
    )
    return jax.shard_map(
        per_device, mesh=mesh, in_specs=placed, out_specs=P("panel", "obs"), check_vma=False
    )
```

time: 226 us -> 55.3 us (0.24)
  waiting for transfers between devices: 92.7 us -> 0 us
  Pallas kernels: 0 us -> 49.2 us
  matrix products: 37.2 us -> 0 us
  loops' own time: 28.7 us -> 0 us
  blocking collectives: 21.3 us -> 0 us
  other arithmetic: 16 us -> 0.79 us
  between operations: 13.5 us -> 0.04 us
  local copies, waits for them, and re-layouts: 14.9 us -> 5.07 us
    all_gather x1 -> x0, waiting for transfers between devices: 75.2 us -> none  [per_device(): group = lax.all_gather(local, 'obs', axis=0, tiled=True)]
    pallas_call x0 -> x1, Pallas kernels: none -> 49.2 us  [per_device(): pl.pallas_call(kernel, out_shape=jax.ShapeDtypeStruct((32, 128), jnp.floa...]
    dot_general x32 -> x0, matrix products: 37.2 us -> none  [the longest x16 19.1 us: one_block(): lax.dot_general(press_b, load_b, dims, preferred_element_type=jnp.float32)]
    another operation x1 -> x0, loops' own time: 28.7 us -> none  [per_device(): lax.scan(one_block, start, (press_blocks, rate_blocks, load_blocks, thick...]
    all_to_all x1 -> x0, blocking collectives: 21.3 us -> none  [per_device(): lax.all_to_all(buffer.reshape(count, cap, 2, steps), ('panel', 'obs'), sp...]
    reduce_scatter x1 -> x0, waiting for transfers between devices: 17.5 us -> none  [per_device(): lax.psum_scatter(partial_sum, 'panel', scatter_dimension=0, tiled=True)]
    sub x16 -> x0, other arithmetic: 10.4 us -> none  [delay_block(): start = steps - delay]
    scatter x1 -> x0, local copies, waits for them, and re-layouts: 9.74 us -> none  [per_device(): jnp.zeros((count * cap, 2, steps), les_rows.dtype).at[position]]
  transfers between devices with their start and end apart: 2 -> 0, of which waited for: 2 -> 0; matrix products, arithmetic and copies ran while one was open for 0% -> 0% of each run, Pallas kernels for 0% -> 0%
where the time goes in v2:
time: 55.3 us; the launch traced here: 55.1 us
  Pallas kernels  49.2 us (89%)
  local copies, waits for them, and re-layouts  5.07 us (9%)
  other arithmetic  0.79 us (1%)
    pallas_call x1, Pallas kernels, per_device(): pl.pallas_call(kernel, out_shape=jax.ShapeDtypeStruct((32, 128), jnp.floa...  49.2 us
    unnamed x3, local copies, waits for them, and re-layouts  4.03 us

profile of v2, /device:TPU:1, one launch (start us, length us, event | category | flops | bytes accessed | tf_op | source)
XLA Modules:
  0.0 55.1 jit_solution(9431079391882464101)
XLA Ops:
  0.0 1.0 %fusion.2 = (bf16[128,1,128]{2,1,0:T(2,128)(2,1)S(1)}, bf16[128,1,128]{2,1,0:T(2,128)(2,1)S(1)}) fusion(bf16[128,2,128]{2,1,0:T(2,128)(2,1)} %param.6), kind=kLoop, calls=%fused_computation.7 | loop fusion | bytes 131072 | tf_op jit(solution)/shard_map/slice | solution.py:345
  1.1 0.1 pad_convert_fusion
  1.1 0.1 fusion.1
  1.2 0.6 %pad_maximum_fusion.blk_ref = bf16[128,256]{1,0:T(8,128)(2,1)} fusion(bf16[128,128]{1,0:T(8,128)(2,1)S(1)} %fusion.1, bf16[128,128]{1,0:T(8,128)(2,1)S(1)} %get-tuple-element.8), kind=kLoop, calls=%fused_computation.3 | loop fusion | flops 131072 | bytes 131072 | tf_op jit(solution)/shard_map/concatenate | solution.py:345
  1.9 1.4 %copy.9.dest_ref = s32[128,1]{1,0:T(8,128)} copy(s32[128,1]{0,1:T(1,128)} %param.7) | data formatting | bytes 1024 | tf_op args[1]
  3.2 1.3 %copy.10.delay_ref = s32[16,1]{1,0:T(8,128)} copy(s32[16,1]{0,1:T(1,128)} %param.10) | data formatting | bytes 128 | tf_op args[4]
  4.6 49.2 %shard_map.64 = f32[32,128]{1,0:T(8,128)} custom-call(bf16[128,256]{1,0:T(8,128)(2,1)} %pad_maximum_fusion.blk_ref, s32[256,128]{1,0:T(8,128)} %constant.8.clone.code_ref, s32[128,1]{1,0:T(8,128)} %copy.9.dest_ref, bf16[8192,128]{1,0:T(8,128)(2,1)} %load_ref.1, bf16[8192,128]{1,0:T(8,128)(2,1)} %thick_ref.1, s32[16,1]{1,0:T(8,128)} %copy.10.delay_ref), custom_call_target="tpu_custom_call" | custom-call | tf_op jit(solution)/shard_map/pallas_call | solution.py:355
  53.7 1.3 %copy.16 = f32[32,128]{1,0:T(8,128)} copy(f32[32,128]{1,0:T(8,128)} %shard_map.64) | data formatting | bytes 32768
  (1 shorter events, 0.0 us)
